TPU v7x, 32 devices: a whole 2x2x4 slice. The times are simulated.
32 devices in a mesh: rows: 16 (over z, y, x), cols: 2 (over core).
Axes of the slice: x: 2, y: 2, z: 4, core: 2. Of those that a mesh axis runs over, the one named last changes fastest.
Arguments:
- quantized: bfloat16 [3072, 384, 128], P('rows', 'cols'), may hold values from 0 to 127, as said below
- scales: bfloat16 [3072, 384], P('rows', 'cols'), may hold values from 0 to 1, as said below
- mode_one: float32 [3072, 32], P('rows'), may hold values from 0 to 40
- mode_two: bfloat16 [384, 32], P('cols'), may hold values from 0 to 1, as said below
- mode_three: bfloat16 [4096, 32], replicated, may hold values from 0 to 0.29882812
- core_tensor: float32 [32, 32, 32], P('rows'), may hold values from 0.0002 to 0.004
- slab_index: int32 [1], replicated, may hold values from 0 to 31
Outputs:
- new_one: float32 [3072, 32], P('rows')
- new_core: float32 [32, 32, 32], P('rows')
Inputs may be any that keep to these rules, and one draw needn't show every extreme that they name: `quantized`: nonnegative integer values of an int8 quantization. `scales`: positive. `mode_two`: nonnegative.
All inputs are finite; a program needn't handle non-finite values.
Results may differ from a plain program's by a relative error of at most 0.0017.
Values sent between devices are 32-bit elements; how exact they have to be, the bound alone decides.
A program may use at most 64 MiB of HBM per device.

v0:
```python
import jax
import jax.numpy as jnp
from jax import lax
from jax.sharding import PartitionSpec as P

SLAB = 128


def weight_gram(core_whole, gram_two, gram_three):
    highest = lax.Precision.HIGHEST
    left = jnp.einsum("rab,ac->rcb", core_whole, gram_two, precision=highest)
    left = jnp.einsum("rcb,bd->rcd", left, gram_three, precision=highest)
    flat = core_whole.reshape(core_whole.shape[0], -1)
    return jnp.dot(left.reshape(flat.shape), flat.T, precision=highest)


def hals_sweep(current, target, coupling):
    highest = lax.Precision.HIGHEST

    def column(position, values):
        where = jnp.asarray(position).astype(jnp.int32)
        weights = lax.dynamic_slice_in_dim(coupling, where, 1, 1)[:, 0]
        diagonal = lax.dynamic_index_in_dim(weights, where, 0, keepdims=False)
        wanted = lax.dynamic_slice_in_dim(target, where, 1, 1)[:, 0]
        before = lax.dynamic_slice_in_dim(values, where, 1, 1)[:, 0]
        fitted = jnp.dot(values, weights, precision=highest)
        after = jnp.maximum(before + (wanted - fitted) / diagonal, 0.0)
        return lax.dynamic_update_slice_in_dim(values, after[:, None], where, 1)

    return lax.fori_loop(0, coupling.shape[0], column, current)


def local(quantized, scales, mode_one, mode_two, mode_three, core_tensor, slab_index):
    highest = lax.Precision.HIGHEST
    whole_core = lax.all_gather(core_tensor, "rows", axis=0, tiled=True)
    flat_core = whole_core.reshape(whole_core.shape[0], -1)
    offset = slab_index[0] * SLAB
    chosen = lax.dynamic_slice_in_dim(mode_three, offset, SLAB, 0)
    tensor = quantized * scales[:, :, None]
    folded = jnp.einsum("jr,ijk->irk", mode_two, tensor, preferred_element_type=jnp.float32).astype(
        jnp.bfloat16
    )
    partial_value = jnp.einsum("irk,ks->irs", folded, chosen, preferred_element_type=jnp.float32)
    partial_value = partial_value.reshape(partial_value.shape[0], -1)
    gram_local = jnp.dot(mode_two.T, mode_two, preferred_element_type=jnp.float32)
    gram_three = jnp.dot(chosen.T, chosen, preferred_element_type=jnp.float32)
    local_target = jnp.dot(partial_value, flat_core.T, precision=highest)
    target, gram_two = lax.psum((local_target, gram_local), "cols")
    coupling = weight_gram(whole_core, gram_two, gram_three)
    updated = hals_sweep(mode_one, target, coupling)
    squares = jnp.sum(updated * updated, axis=0)
    counted = mode_one.shape[0] * lax.axis_size("rows")
    totals = lax.psum(squares, "rows")
    spread = jnp.sqrt(totals / counted + 1e-06)
    normed = updated / spread
    local_rank = core_tensor.shape[0]
    owned = lax.dynamic_slice_in_dim(spread, lax.axis_index("rows") * local_rank, local_rank, 0)
    return (normed, core_tensor * owned[:, None, None])


def solution(mesh):
    in_specs = (
        P("rows", "cols", None),
        P("rows", "cols"),
        P("rows", None),
        P("cols", None),
        P(),
        P("rows", None, None),
        P(),
    )
    out_specs = (P("rows", None), P("rows", None, None))
    return jax.shard_map(local, mesh=mesh, in_specs=in_specs, out_specs=out_specs, check_vma=False)
```

profile of v0, /device:TPU:0, one launch (start us, length us, event | category | flops | bytes accessed | tf_op | source)
XLA Modules:
  0.0 148.8 jit_solution(15536030878287488232)
XLA Ops:
  1.4 8.6 %fusion.10 = bf16[192,32,128]{2,1,0:T(8,128)(2,1)S(1)} fusion(bf16[192,192,128]{2,1,0:T(8,128)(2,1)} %param.9, bf16[192,192]{1,0:T(8,128)(2,1)} %param.10, bf16[192,32]{0,1:T(8,128)(2,1)} %param.12), kind=kOutput, calls=%fused_computation.12 | convolution fusion | flops 321650688 | bytes 11096064 | tf_op jit(solution)/shard_map/jr,ijk->irk/dot_general | solution.py:40
  10.0 1.1 fusion.8
  11.1 45.3 %all_gather.3 = f32[32,32,32]{2,1,0:T(8,128)S(1)} all-gather(f32[2,32,32]{2,1,0:T(8,128)S(1)} %copy-done.2), channel_id=1, replica_groups=mesh['rows'=16,'cols'=2] {'rows'}, dimensions={0}, use_global_device_ids=true | all-gather | bytes 139264 | tf_op jit(solution)/shard_map/all_gather | solution.py:35
  56.5 1.1 convolution_bitcast_fusion.1
  57.7 3.5 %all-reduce = (f32[192,32]{0,1:T(8,128)S(1)}, f32[32,32]{1,0:T(8,128)S(1)}) all-reduce(f32[192,32]{0,1:T(8,128)S(1)} %convolution_bitcast_fusion.1, f32[32,32]{1,0:T(8,128)S(1)} %fusion.24), channel_id=1, replica_groups=mesh['rows'=16,'cols'=2] {'cols'}, use_global_device_ids=true, to_apply=%region_1.0 | all-reduce | flops 7168 | bytes 57344 | tf_op jit(solution)/shard_map/psum | solution.py:48
  62.0 0.9 fusion.13
  62.9 0.8 convolution_bitcast_fusion.2
  63.7 46.9 %while.16 = (s32[]{:T(128)}, f32[192,32]{0,1:T(8,128)S(1)}, f32[192,32]{0,1:T(8,128)S(1)}, f32[32,32]{0,1:T(8,128)S(1)}, s32[]{:T(128)}, /*index=5*/s32[]{:T(128)}, s32[]{:T(128)}) while((s32[]{:T(128)}, f32[192,32]{0,1:T(8,128)S(1)}, f32[192,32]{0,1:T(8,128)S(1)}, f32[32,32]{0,1:T(8,128)S(1)}, s32[]{:T(128)}, /*index=5*/s32[]{:T(128)}, ...), condition=%wide.region_3.4_spmd, body=%wide.region_2.3_spmd.sunk | while | flops 74499 | bytes 41849 | solution.py:30
  64.5 0.7 fusion.37
  65.9 0.7 fusion.37
  67.4 0.7 fusion.37
  68.9 0.7 fusion.37
  70.3 0.7 fusion.37
  71.8 0.7 fusion.37
  73.3 0.7 fusion.37
  74.7 0.7 fusion.37
  76.2 0.7 fusion.37
  77.7 0.7 fusion.37
  79.1 0.7 fusion.37
  80.6 0.7 fusion.37
  82.1 0.7 fusion.37
  83.5 0.7 fusion.37
  85.0 0.7 fusion.37
  86.5 0.7 fusion.37
  88.0 0.7 fusion.37
  95.3 0.7 fusion.37
  96.8 0.7 fusion.37
  98.2 0.7 fusion.37
  110.0 0.7 fusion.37
  110.8 36.6 %psum.23 = f32[32]{0:T(128)S(1)} all-reduce(f32[32]{0:T(128)S(1)} %multiply_reduce_fusion), channel_id=1, replica_groups=mesh['rows'=16,'cols'=2] {'rows'}, use_global_device_ids=true, to_apply=%region_5.6 | all-reduce | flops 32 | bytes 256 | tf_op jit(solution)/shard_map/psum | solution.py:53
  147.4 0.7 broadcast_divide_fusion
  148.1 0.7 broadcast_multiply_fusion
  (153 shorter events, 33.2 us)
Async XLA Ops:
  0.6 9.4 %copy-start = (bf16[4096,32]{0,1:T(8,128)(2,1)S(1)}, bf16[4096,32]{0,1:T(8,128)(2,1)}, u32[]{:S(2)}) copy-start(bf16[4096,32]{0,1:T(8,128)(2,1)} %param.13) | copy-start | bytes 786436
  0.6 56.9 %copy-start.3 = (bf16[192,32]{0,1:T(8,128)(2,1)S(1)}, bf16[192,32]{0,1:T(8,128)(2,1)}, u32[]{:S(2)}) copy-start(bf16[192,32]{0,1:T(8,128)(2,1)} %param.12) | copy-start | bytes 36868
  0.7 10.5 %copy-start.2 = (f32[2,32,32]{2,1,0:T(8,128)S(1)}, f32[2,32,32]{2,1,0:T(8,128)}, u32[]{:S(2)}) copy-start(f32[2,32,32]{2,1,0:T(8,128)} %param.14) | copy-start | bytes 24580
  1.4 62.4 %copy-start.1 = (f32[192,32]{0,1:T(8,128)S(1)}, f32[192,32]{0,1:T(8,128)}, u32[]{:S(2)}) copy-start(f32[192,32]{0,1:T(8,128)} %param.11) | copy-start | bytes 73732
where the time goes:
time: 149 us
  blocking collectives  85.5 us (57%)
  other arithmetic  22.3 us (15%)
  local copies, waits for them, and re-layouts  20.7 us (14%)
  matrix products  17.8 us (12%)
    all_gather x1, blocking collectives, local(): whole_core = lax.all_gather(core_tensor, 'rows', axis=0, tiled=True)  45.3 us
    psum x1, blocking collectives, local(): totals = lax.psum(squares, 'rows')  36.6 us
    max x32, other arithmetic, column(): after = jnp.maximum(before + (wanted - fitted) / diagonal, 0.0)  20.8 us
    dynamic_slice x32, local copies, waits for them, and re-layouts, column(): diagonal = lax.dynamic_index_in_dim(weights, where, 0, keepdims=False)  18.9 us
    dot_general x1, matrix products, local(): jnp.einsum('jr,ijk->irk', mode_two, tensor, preferred_element_type=jnp.fl...  8.62 us
    dot_general x32, matrix products, column(): fitted = jnp.dot(values, weights, precision=highest)  4.4 us
    psum x1, blocking collectives, local(): target, gram_two = lax.psum((local_target, gram_local), 'cols')  3.54 us

commit v1 on v0

v1 whole, which is shorter than its diff:
```python
import functools

import jax
import jax.numpy as jnp
from jax import lax
from jax.experimental import pallas as pl
from jax.experimental.pallas import tpu as pltpu
from jax.sharding import PartitionSpec as P

SLAB = 128
GROUP = 8
STEP = 32
MESH = pl.DeviceIdType.MESH
HIGHEST = lax.Precision.HIGHEST
NT = (((1,), (1,)), ((), ()))
TN = (((0,), (0,)), ((), ()))


def swap_blocks(parts):
    axis = parts[0].ndim - 1
    lane = lax.broadcasted_iota(jnp.int32, parts[0].shape, axis)
    for bit, shift in ((1, 32), (2, 64)):
        low = (lane & shift) == 0
        out = [None] * 4
        for b in range(4):
            if b & bit:
                continue
            x, y = parts[b], parts[b | bit]
            out[b] = jnp.where(low, x, pltpu.roll(y, shift, axis))
            out[b | bit] = jnp.where(low, pltpu.roll(x, 128 - shift, axis), y)
        parts = out
    return parts


def kernel(
    n_rows, n_cols, slab_ref, q_hbm, scales_ref, one_ref, two_ref, three_ref, core_ref,
    new_one_ref, new_core_ref,
    q_ref, bd_ref, pick_ref, pf_ref, cf_ref, yf_ref, gram_ref, target_ref, square_ref,
    q_sem, core_send, core_recv, gram_send, gram_recv, target_send, target_recv, sq_send, sq_recv,
):
    row, col = lax.axis_index("rows"), lax.axis_index("cols")
    n_i, n_j = scales_ref.shape
    own = core_ref.shape[0]
    rank = two_ref.shape[0]
    chunks = n_i // STEP
    wide = GROUP * rank

    def chunk_copy(c):
        rows = pl.ds(pl.multiple_of(c * STEP, STEP), STEP)
        return pltpu.make_async_copy(q_hbm.at[rows], q_ref.at[rows], q_sem.at[c])

    for c in range(chunks):
        chunk_copy(c).start()

    barrier = pltpu.get_barrier_semaphore()
    for d in range(1, n_rows):
        pl.semaphore_signal(
            barrier, inc=1, device_id={"rows": lax.rem(row + d, n_rows), "cols": col}, device_id_type=MESH
        )
    for d in range(1, n_cols):
        pl.semaphore_signal(
            barrier, inc=1, device_id={"rows": row, "cols": lax.rem(col + d, n_cols)}, device_id_type=MESH
        )

    def push(ref, size, send, recv, axis, d):
        count, me = (n_rows, row) if axis == "rows" else (n_cols, col)
        peer = lax.rem(me + d, count)
        where = {"rows": peer, "cols": col} if axis == "rows" else {"rows": row, "cols": peer}
        slot = ref.at[pl.ds(pl.multiple_of(me * size, size), size), :]
        return pltpu.make_async_remote_copy(
            src_ref=slot, dst_ref=slot, send_sem=send.at[d], recv_sem=recv.at[d], device_id=where, device_id_type=MESH
        )

    wanted = jnp.full((rank, SLAB), slab_ref[0], jnp.int32)
    chosen_t = jnp.zeros((rank, SLAB), jnp.float32)
    for n in range(three_ref.shape[1] // SLAB):
        piece = three_ref[:, n * SLAB : (n + 1) * SLAB].astype(jnp.float32)
        chosen_t = jnp.where(wanted == n, piece, chosen_t)
    chosen = chosen_t.T.astype(jnp.bfloat16)
    chosen_t = chosen_t.astype(jnp.bfloat16)
    two = two_ref[...]
    tiled = jnp.concatenate([chosen] * GROUP, axis=1)
    block = lax.broadcasted_iota(jnp.int32, tiled.shape, 1) // rank
    for t in range(GROUP):
        bd_ref[t * SLAB : (t + 1) * SLAB, :] = jnp.where(block == t, tiled, jnp.zeros_like(tiled))
    which = lax.broadcasted_iota(jnp.int32, pick_ref.shape, 1) // rank
    pick_ref[...] = jnp.where(
        which == lax.broadcasted_iota(jnp.int32, pick_ref.shape, 0), 1.0, 0.0
    ).astype(jnp.bfloat16)
    for q in range(own):
        packed = jnp.concatenate([core_ref[q, 8 * b : 8 * b + 8, :] for b in range(4)], axis=1)
        cf_ref[pl.ds(pl.multiple_of((row * own + q) * 8, 8), 8), :] = packed
    gram = lax.dot_general(two, two, NT, preferred_element_type=jnp.float32)
    gram_ref[pl.ds(pl.multiple_of(col * rank, rank), rank), :] = gram

    pl.semaphore_wait(barrier, n_rows + n_cols - 2)
    cores = [push(cf_ref, 8 * own, core_send, core_recv, "rows", d) for d in range(1, n_rows)]
    grams = [push(gram_ref, rank, gram_send, gram_recv, "cols", d) for d in range(1, n_cols)]
    for copy in grams + cores:
        copy.start()

    def chunk(c, carry):
        chunk_copy(c).wait()
        base = pl.multiple_of(c * STEP, STEP)
        spread_scales = lax.dot_general(
            scales_ref[pl.ds(base, STEP), :], pick_ref[...], TN, preferred_element_type=jnp.float32
        )
        lhs = jnp.concatenate(
            [
                jnp.concatenate([q_ref[base + g * GROUP + t] for t in range(GROUP)], axis=1)
                for g in range(STEP // GROUP)
            ],
            axis=0,
        )
        projected = jnp.dot(lhs, bd_ref[...], preferred_element_type=jnp.float32)
        for g in range(STEP // GROUP):
            scaled = projected[g * n_j : (g + 1) * n_j] * spread_scales[:, g * wide : (g + 1) * wide]
            partial = jnp.dot(two, scaled.astype(jnp.bfloat16), preferred_element_type=jnp.float32)
            for h in range(wide // 128):
                turned = swap_blocks([partial[8 * b : 8 * b + 8, 128 * h : 128 * h + 128] for b in range(4)])
                start = pl.multiple_of((base + g * GROUP + 4 * h) * 8, 32)
                pf_ref[pl.ds(start, 32), :] = jnp.concatenate(turned, axis=0)
        return carry

    lax.fori_loop(0, chunks, chunk, 0)

    for copy in cores:
        copy.wait_recv()

    def flat(ref, count):
        return jnp.concatenate([ref[pl.ds(a, count, stride=8), :] for a in range(8)], axis=1)

    core_flat = flat(cf_ref, rank)
    target_ref[pl.ds(pl.multiple_of(col * rank, rank), rank), :] = lax.dot_general(
        core_flat, flat(pf_ref, n_i), NT, preferred_element_type=jnp.float32, precision=HIGHEST
    )
    targets = [push(target_ref, rank, target_send, target_recv, "cols", d) for d in range(1, n_cols)]
    for copy in targets:
        copy.start()

    quad = jnp.concatenate([chosen_t] * 4, axis=0)
    gram_three = lax.dot_general(quad, quad, NT, preferred_element_type=jnp.float32)
    same = lax.broadcasted_iota(jnp.int32, gram_three.shape, 0) // rank == (
        lax.broadcasted_iota(jnp.int32, gram_three.shape, 1) // rank
    )
    gram_three = jnp.where(same, gram_three, 0.0)
    for copy in grams:
        copy.wait_recv()
    gram_two = sum(gram_ref[c * rank : (c + 1) * rank, :] for c in range(1, n_cols)) + gram_ref[0:rank, :]
    left = jnp.dot(cf_ref[...], gram_three, preferred_element_type=jnp.float32, precision=HIGHEST)
    stacked = []
    for g in range(rank // 4):
        stacked.append(
            jnp.concatenate(swap_blocks([left[32 * g + 8 * t : 32 * g + 8 * t + 8] for t in range(4)]), axis=0)
        )
    left = jnp.dot(
        gram_two, jnp.concatenate(stacked, axis=1), preferred_element_type=jnp.float32, precision=HIGHEST
    )
    for g in range(rank // 4):
        back = swap_blocks([left[8 * b : 8 * b + 8, 128 * g : 128 * g + 128] for b in range(4)])
        yf_ref[32 * g : 32 * g + 32, :] = jnp.concatenate(back, axis=0)
    coupling = lax.dot_general(
        flat(yf_ref, rank), core_flat, NT, preferred_element_type=jnp.float32, precision=HIGHEST
    )
    diagonal = lax.broadcasted_iota(jnp.int32, coupling.shape, 0) == lax.broadcasted_iota(jnp.int32, coupling.shape, 1)
    inverse = 1.0 / jnp.sum(jnp.where(diagonal, coupling, 0.0), axis=1, keepdims=True)
    current = one_ref[...]
    fitted = jnp.dot(coupling, current, preferred_element_type=jnp.float32, precision=HIGHEST)
    weights = coupling * inverse

    for copy in targets:
        copy.wait_recv()
    target = target_ref[0:rank, :]
    for c in range(1, n_cols):
        target = target + target_ref[c * rank : (c + 1) * rank, :]
    residual = (target - fitted) * inverse

    tiles = [residual[8 * b : 8 * b + 8] for b in range(rank // 8)]
    changes = []
    for q in range(rank):
        b, a = divmod(q, 8)
        change = jnp.maximum(tiles[b][a : a + 1], -current[q : q + 1])
        changes.append(change)
        for k in range(b, rank // 8):
            tiles[k] = tiles[k] - weights[8 * k : 8 * k + 8, q : q + 1] * change
    updated = jnp.maximum(current + jnp.concatenate(changes, axis=0), 0.0)

    squares = jnp.sum(updated * updated, axis=1, keepdims=True)
    lane = lax.broadcasted_iota(jnp.int32, (8, 128), 1)
    packed = jnp.zeros((8, 128), jnp.float32)
    for b in range(rank // 8):
        packed = jnp.where(lane == b, squares[8 * b : 8 * b + 8], packed)
    square_ref[pl.ds(pl.multiple_of(row * 8, 8), 8), :] = packed
    sums = [push(square_ref, 8, sq_send, sq_recv, "rows", d) for d in range(1, n_rows)]
    for copy in sums:
        copy.start()
    for copy in sums:
        copy.wait_recv()
    totals = square_ref[0:8, :]
    for r in range(1, n_rows):
        totals = totals + square_ref[8 * r : 8 * r + 8, :]
    spread = jnp.sqrt(totals / (n_i * n_rows) + 1e-06)
    for b in range(rank // 8):
        new_one_ref[8 * b : 8 * b + 8, :] = updated[8 * b : 8 * b + 8] / spread[:, b : b + 1]
    place = lax.broadcasted_iota(jnp.int32, (8, 128), 0) + 8 * lane
    for q in range(own):
        mine = jnp.where(place == row * own + q, spread, 0.0)
        mine = jnp.sum(jnp.sum(mine, axis=1, keepdims=True), axis=0, keepdims=True)
        new_core_ref[q] = core_ref[q] * mine
    for copy in cores + grams + targets + sums:
        copy.wait_send()


def local(n_rows, n_cols, quantized, scales, mode_one, mode_two, mode_three, core_tensor, slab_index):
    n_i, n_j, _ = quantized.shape
    rank = mode_two.shape[1]
    own = core_tensor.shape[0]
    f32, bf16 = jnp.float32, jnp.bfloat16
    vmem = pl.BlockSpec(memory_space=pltpu.VMEM)
    dma = pltpu.SemaphoreType.DMA
    one_t, new_core = pl.pallas_call(
        functools.partial(kernel, n_rows, n_cols),
        out_shape=(
            jax.ShapeDtypeStruct((rank, n_i), f32),
            jax.ShapeDtypeStruct((own, rank, rank), f32),
        ),
        in_specs=[pl.BlockSpec(memory_space=pltpu.SMEM), pl.BlockSpec(memory_space=pl.ANY)] + [vmem] * 5,
        out_specs=(vmem, vmem),
        scratch_shapes=[
            pltpu.VMEM(quantized.shape, bf16),
            pltpu.VMEM((GROUP * SLAB, GROUP * rank), bf16),
            pltpu.VMEM((STEP, STEP * rank), bf16),
            pltpu.VMEM((n_i * 8, 128), f32),
            pltpu.VMEM((rank * 8, 128), f32),
            pltpu.VMEM((rank * 8, 128), f32),
            pltpu.VMEM((n_cols * rank, rank), f32),
            pltpu.VMEM((n_cols * rank, n_i), f32),
            pltpu.VMEM((n_rows * 8, 128), f32),
            dma((n_i // STEP,)),
            dma((n_rows,)),
            dma((n_rows,)),
            dma((n_cols,)),
            dma((n_cols,)),
            dma((n_cols,)),
            dma((n_cols,)),
            dma((n_rows,)),
            dma((n_rows,)),
        ],
        compiler_params=pltpu.CompilerParams(
            collective_id=0, has_side_effects=True, vmem_limit_bytes=40 * 1024 * 1024
        ),
    )(slab_index, quantized, scales, mode_one.T, mode_two.T, mode_three.T, core_tensor)
    return one_t.T, new_core


def solution(mesh):
    in_specs = (
        P("rows", "cols", None),
        P("rows", "cols"),
        P("rows", None),
        P("cols", None),
        P(),
        P("rows", None, None),
        P(),
    )
    out_specs = (P("rows", None), P("rows", None, None))
    return jax.shard_map(
        functools.partial(local, mesh.shape["rows"], mesh.shape["cols"]),
        mesh=mesh,
        in_specs=in_specs,
        out_specs=out_specs,
        check_vma=False,
    )
```

time: 149 us -> 32 us (0.21)
  blocking collectives: 85.5 us -> 0 us
  other arithmetic: 22.3 us -> 0 us
  Pallas kernels: 0 us -> 21.3 us
  matrix products: 17.8 us -> 0 us
  local copies, waits for them, and re-layouts: 20.7 us -> 8.98 us
    all_gather x1 -> x0, blocking collectives: 45.3 us -> none  [local(): whole_core = lax.all_gather(core_tensor, 'rows', axis=0, tiled=True)]
    psum x2 -> x0, blocking collectives: 40.1 us -> none  [the longest x1 36.6 us: local(): totals = lax.psum(squares, 'rows')]
    pallas_call x0 -> x1, Pallas kernels: none -> 21.3 us  [local(): pl.pallas_call(functools.partial(kernel, n_rows, n_cols), out_shape=(jax....]
    max x32 -> x0, other arithmetic: 20.8 us -> none  [column(): after = jnp.maximum(before + (wanted - fitted) / diagonal, 0.0)]
    dynamic_slice x65 -> x0, local copies, waits for them, and re-layouts: 19.3 us -> none  [the longest x32 18.9 us: column(): diagonal = lax.dynamic_index_in_dim(weights, where, 0, keepdims=False)]
    dot_general x40 -> x0, matrix products: 17.8 us -> none  [the longest x1 8.62 us: local(): jnp.einsum('jr,ijk->irk', mode_two, tensor, preferred_element_type=jnp.fl...]
    unnamed x8 -> x14, local copies, waits for them, and re-layouts: 0.02 us -> 8.98 us
where the time goes in v1:
time: 32 us; the launch traced here: 31.6 us
  Pallas kernels  21.3 us (67%)
  local copies, waits for them, and re-layouts  8.98 us (28%)
  between operations  1.3 us (4%)
    pallas_call x1, Pallas kernels, local(): pl.pallas_call(functools.partial(kernel, n_rows, n_cols), out_shape=(jax....  21.3 us
    unnamed x14, local copies, waits for them, and re-layouts  8.98 us

profile of v1, /device:TPU:0, one launch (start us, length us, event | category | flops | bytes accessed | tf_op | source)
XLA Modules:
  0.0 31.6 jit_solution(16238582164876651026)
XLA Ops:
  1.3 0.0 copy-start
  1.3 3.7 %copy-done = bf16[192,192,128]{2,1,0:T(8,128)(2,1)S(1)} copy-done((bf16[192,192,128]{2,1,0:T(8,128)(2,1)S(1)}, bf16[192,192,128]{2,1,0:T(8,128)(2,1)}, u32[]{:S(2)}) %copy-start) | copy-done | bytes 9437208
  5.0 0.0 copy-start.1
  5.0 0.9 %copy-done.1 = bf16[4096,32]{0,1:T(8,128)(2,1)S(1)} copy-done((bf16[4096,32]{0,1:T(8,128)(2,1)S(1)}, bf16[4096,32]{0,1:T(8,128)(2,1)}, u32[]{:S(2)}) %copy-start.1) | copy-done | bytes 262168
  5.9 0.0 copy-start.2
  5.9 0.9 %copy-done.2 = bf16[192,192]{1,0:T(8,128)(2,1)S(1)} copy-done((bf16[192,192]{1,0:T(8,128)(2,1)S(1)}, bf16[192,192]{1,0:T(8,128)(2,1)}, u32[]{:S(2)}) %copy-start.2) | copy-done | bytes 73752
  6.8 0.0 copy-start.3
  6.8 0.8 %copy-done.3 = f32[192,32]{0,1:T(8,128)S(1)} copy-done((f32[192,32]{0,1:T(8,128)S(1)}, f32[192,32]{0,1:T(8,128)}, u32[]{:S(2)}) %copy-start.3) | copy-done | bytes 24600
  7.6 0.0 copy-start.4
  7.6 0.8 %copy-done.4 = f32[2,32,32]{2,1,0:T(8,128)S(1)} copy-done((f32[2,32,32]{2,1,0:T(8,128)S(1)}, f32[2,32,32]{2,1,0:T(8,128)}, u32[]{:S(2)}) %copy-start.4) | copy-done | bytes 8216
  8.3 0.0 copy-start.5
  8.3 0.7 %copy-done.5 = bf16[192,32]{0,1:T(8,128)(2,1)S(1)} copy-done((bf16[192,32]{0,1:T(8,128)(2,1)S(1)}, bf16[192,32]{0,1:T(8,128)(2,1)}, u32[]{:S(2)}) %copy-start.5) | copy-done | bytes 12312
  9.0 21.3 %shard_map.86 = (f32[32,192]{1,0:T(8,128)S(1)}, f32[2,32,32]{2,1,0:T(8,128)S(1)}) custom-call(s32[1]{0:T(128)S(6)} %copy.11.slab_ref, bf16[192,192,128]{2,1,0:T(8,128)(2,1)S(1)} %copy-done, bf16[192,192]{1,0:T(8,128)(2,1)S(1)} %copy-done.2, f32[32,192]{1,0:T(8,128)S(1)} %bitcast.5, bf16[32,192]{1,0:T(8,128)(2,1)S(1)} %bitcast.7, ...), custom_call_target="tpu_custom_call" | custom-call | tf_op jit(solution)/shard_map/pallas_call | solution.py:221
  30.4 0.6 %copy.12 = f32[192,32]{0,1:T(8,128)} copy(f32[192,32]{0,1:T(8,128)S(1)} %bitcast.6) | data formatting | bytes 49152
  31.0 0.6 %copy.13 = f32[2,32,32]{2,1,0:T(8,128)} copy(f32[2,32,32]{2,1,0:T(8,128)S(1)} %get-tuple-element.9) | data formatting | bytes 16384
Async XLA Ops:
  1.3 3.7 %copy-start = (bf16[192,192,128]{2,1,0:T(8,128)(2,1)S(1)}, bf16[192,192,128]{2,1,0:T(8,128)(2,1)}, u32[]{:S(2)}) copy-start(bf16[192,192,128]{2,1,0:T(8,128)(2,1)} %q_hbm.1) | copy-start | bytes 28311556
  5.0 0.9 %copy-start.1 = (bf16[4096,32]{0,1:T(8,128)(2,1)S(1)}, bf16[4096,32]{0,1:T(8,128)(2,1)}, u32[]{:S(2)}) copy-start(bf16[4096,32]{0,1:T(8,128)(2,1)} %param.11) | copy-start | bytes 786436
  5.9 0.9 %copy-start.2 = (bf16[192,192]{1,0:T(8,128)(2,1)S(1)}, bf16[192,192]{1,0:T(8,128)(2,1)}, u32[]{:S(2)}) copy-start(bf16[192,192]{1,0:T(8,128)(2,1)} %scales_ref.1) | copy-start | bytes 221188
  6.8 0.8 %copy-start.3 = (f32[192,32]{0,1:T(8,128)S(1)}, f32[192,32]{0,1:T(8,128)}, u32[]{:S(2)}) copy-start(f32[192,32]{0,1:T(8,128)} %param.9) | copy-start | bytes 73732
  7.6 0.8 %copy-start.4 = (f32[2,32,32]{2,1,0:T(8,128)S(1)}, f32[2,32,32]{2,1,0:T(8,128)}, u32[]{:S(2)}) copy-start(f32[2,32,32]{2,1,0:T(8,128)} %core_ref.1) | copy-start | bytes 24580
  8.3 0.7 %copy-start.5 = (bf16[192,32]{0,1:T(8,128)(2,1)S(1)}, bf16[192,32]{0,1:T(8,128)(2,1)}, u32[]{:S(2)}) copy-start(bf16[192,32]{0,1:T(8,128)(2,1)} %param.10) | copy-start | bytes 36868

commit v2 on v1

--- a/solution.py
+++ b/solution.py
@@ -33,10 +33,10 @@
 
 
 def kernel(
-    n_rows, n_cols, slab_ref, q_hbm, scales_ref, one_ref, two_ref, three_ref, core_ref,
+    n_rows, n_cols, slab_ref, q_hbm, scales_hbm, one_hbm, two_hbm, three_hbm, core_hbm,
     new_one_ref, new_core_ref,
-    q_ref, bd_ref, pick_ref, pf_ref, cf_ref, yf_ref, gram_ref, target_ref, square_ref,
-    q_sem, core_send, core_recv, gram_send, gram_recv, target_send, target_recv, sq_send, sq_recv,
+    scales_ref, one_ref, two_ref, three_ref, core_ref, q_ref, bd_ref, pick_ref, pf_ref, cf_ref, yf_ref, gram_ref, target_ref, square_ref,
+    in_sem, q_sem, core_send, core_recv, gram_send, gram_recv, target_send, target_recv, sq_send, sq_recv,
 ):
     row, col = lax.axis_index("rows"), lax.axis_index("cols")
     n_i, n_j = scales_ref.shape
@@ -49,9 +49,6 @@
         rows = pl.ds(pl.multiple_of(c * STEP, STEP), STEP)
         return pltpu.make_async_copy(q_hbm.at[rows], q_ref.at[rows], q_sem.at[c])
 
-    for c in range(chunks):
-        chunk_copy(c).start()
-
     barrier = pltpu.get_barrier_semaphore()
     for d in range(1, n_rows):
         pl.semaphore_signal(
@@ -61,6 +58,23 @@
         pl.semaphore_signal(
             barrier, inc=1, device_id={"rows": row, "cols": lax.rem(col + d, n_cols)}, device_id_type=MESH
         )
+
+    small = [
+        pltpu.make_async_copy(src, dst, in_sem.at[n])
+        for n, (src, dst) in enumerate(
+            (
+                (core_hbm, core_ref),
+                (three_hbm, three_ref),
+                (two_hbm, two_ref),
+                (scales_hbm, scales_ref),
+                (one_hbm, one_ref),
+            )
+        )
+    ]
+    for copy in small:
+        copy.start()
+    for c in range(chunks):
+        chunk_copy(c).start()
 
     def push(ref, size, send, recv, axis, d):
         count, me = (n_rows, row) if axis == "rows" else (n_cols, col)
@@ -71,6 +85,16 @@
             src_ref=slot, dst_ref=slot, send_sem=send.at[d], recv_sem=recv.at[d], device_id=where, device_id_type=MESH
         )
 
+    which = lax.broadcasted_iota(jnp.int32, pick_ref.shape, 1) // rank
+    pick_ref[...] = jnp.where(
+        which == lax.broadcasted_iota(jnp.int32, pick_ref.shape, 0), 1.0, 0.0
+    ).astype(jnp.bfloat16)
+    small[0].wait()
+    for q in range(own):
+        packed = jnp.concatenate([core_ref[q, 8 * b : 8 * b + 8, :] for b in range(4)], axis=1)
+        cf_ref[pl.ds(pl.multiple_of((row * own + q) * 8, 8), 8), :] = packed
+    for copy in small[1:]:
+        copy.wait()
     wanted = jnp.full((rank, SLAB), slab_ref[0], jnp.int32)
     chosen_t = jnp.zeros((rank, SLAB), jnp.float32)
     for n in range(three_ref.shape[1] // SLAB):
@@ -83,13 +107,6 @@
     block = lax.broadcasted_iota(jnp.int32, tiled.shape, 1) // rank
     for t in range(GROUP):
         bd_ref[t * SLAB : (t + 1) * SLAB, :] = jnp.where(block == t, tiled, jnp.zeros_like(tiled))
-    which = lax.broadcasted_iota(jnp.int32, pick_ref.shape, 1) // rank
-    pick_ref[...] = jnp.where(
-        which == lax.broadcasted_iota(jnp.int32, pick_ref.shape, 0), 1.0, 0.0
-    ).astype(jnp.bfloat16)
-    for q in range(own):
-        packed = jnp.concatenate([core_ref[q, 8 * b : 8 * b + 8, :] for b in range(4)], axis=1)
-        cf_ref[pl.ds(pl.multiple_of((row * own + q) * 8, 8), 8), :] = packed
     gram = lax.dot_general(two, two, NT, preferred_element_type=jnp.float32)
     gram_ref[pl.ds(pl.multiple_of(col * rank, rank), rank), :] = gram
 
@@ -224,9 +241,14 @@
             jax.ShapeDtypeStruct((rank, n_i), f32),
             jax.ShapeDtypeStruct((own, rank, rank), f32),
         ),
-        in_specs=[pl.BlockSpec(memory_space=pltpu.SMEM), pl.BlockSpec(memory_space=pl.ANY)] + [vmem] * 5,
+        in_specs=[pl.BlockSpec(memory_space=pltpu.SMEM)] + [pl.BlockSpec(memory_space=pl.ANY)] * 6,
         out_specs=(vmem, vmem),
         scratch_shapes=[
+            pltpu.VMEM(scales.shape, bf16),
+            pltpu.VMEM((rank, n_i), f32),
+            pltpu.VMEM((rank, n_j), bf16),
+            pltpu.VMEM((rank, mode_three.shape[0]), bf16),
+            pltpu.VMEM(core_tensor.shape, f32),
             pltpu.VMEM(quantized.shape, bf16),
             pltpu.VMEM((GROUP * SLAB, GROUP * rank), bf16),
             pltpu.VMEM((STEP, STEP * rank), bf16),
@@ -236,6 +258,7 @@
             pltpu.VMEM((n_cols * rank, rank), f32),
             pltpu.VMEM((n_cols * rank, n_i), f32),
             pltpu.VMEM((n_rows * 8, 128), f32),
+            dma((5,)),
             dma((n_i // STEP,)),
             dma((n_rows,)),
             dma((n_rows,)),
@@ -247,7 +270,7 @@
             dma((n_rows,)),
         ],
         compiler_params=pltpu.CompilerParams(
-            collective_id=0, has_side_effects=True, vmem_limit_bytes=40 * 1024 * 1024
+            collective_id=0, has_side_effects=True, vmem_limit_bytes=64 * 1024 * 1024
         ),
     )(slab_index, quantized, scales, mode_one.T, mode_two.T, mode_three.T, core_tensor)
     return one_t.T, new_core

time: 32 us -> 26.9 us (0.84)
  local copies, waits for them, and re-layouts: 8.98 us -> 2.75 us
  Pallas kernels: 21.3 us -> 22.6 us
    unnamed x14 -> x2, local copies, waits for them, and re-layouts: 8.98 us -> 2.75 us
    pallas_call x1, Pallas kernels: 21.3 us -> 22.6 us  [local(): pl.pallas_call(functools.partial(kernel, n_rows, n_cols), out_shape=(jax....]
where the time goes in v2:
time: 26.9 us; the launch traced here: 26.7 us
  Pallas kernels  22.6 us (84%)
  local copies, waits for them, and re-layouts  2.75 us (10%)
  between operations  1.29 us (5%)
    pallas_call x1, Pallas kernels, local(): pl.pallas_call(functools.partial(kernel, n_rows, n_cols), out_shape=(jax....  22.6 us
    unnamed x2, local copies, waits for them, and re-layouts  2.75 us

profile of v2, /device:TPU:0, one launch (start us, length us, event | category | flops | bytes accessed | tf_op | source)
XLA Modules:
  0.0 26.7 jit_solution(1106527467624667879)
XLA Ops:
  1.3 22.6 %shard_map.86 = (f32[32,192]{1,0:T(8,128)}, f32[2,32,32]{2,1,0:T(8,128)}) custom-call(s32[1]{0:T(128)S(6)} %copy.11.slab_ref, bf16[192,192,128]{2,1,0:T(8,128)(2,1)} %q_hbm.1, bf16[192,192]{1,0:T(8,128)(2,1)} %scales_hbm.1, f32[32,192]{1,0:T(8,128)} %bitcast.5, bf16[32,192]{1,0:T(8,128)(2,1)} %bitcast.7, bf16[32,4096]{1,0:T(8,128)(2,1)} %bitcast.4, ...), custom_call_target="tpu_custom_call" | custom-call | tf_op jit(solution)/shard_map/pallas_call | solution.py:238
  23.9 1.4 %copy.12 = f32[192,32]{0,1:T(8,128)} copy(f32[192,32]{0,1:T(8,128)} %bitcast.6) | data formatting | bytes 49152
  25.3 1.4 %copy.13 = f32[2,32,32]{2,1,0:T(8,128)} copy(f32[2,32,32]{2,1,0:T(8,128)} %get-tuple-element.9) | data formatting | bytes 16384

commit v3 on v2

--- a/solution.py
+++ b/solution.py
@@ -32,16 +32,21 @@
     return parts
 
 
+def flip(index, bit):
+    return index + bit - 2 * bit * lax.rem(index // bit, 2)
+
+
 def kernel(
     n_rows, n_cols, slab_ref, q_hbm, scales_hbm, one_hbm, two_hbm, three_hbm, core_hbm,
     new_one_ref, new_core_ref,
-    scales_ref, one_ref, two_ref, three_ref, core_ref, q_ref, bd_ref, pick_ref, pf_ref, cf_ref, yf_ref, gram_ref, target_ref, square_ref,
+    scales_ref, one_ref, two_ref, three_ref, core_ref, q_ref, bd_ref, pick_ref, pf_ref, cf_ref, core_all_ref, yf_ref, gram_ref, target_ref, square_ref,
     in_sem, q_sem, core_send, core_recv, gram_send, gram_recv, target_send, target_recv, sq_send, sq_recv,
 ):
     row, col = lax.axis_index("rows"), lax.axis_index("cols")
     n_i, n_j = scales_ref.shape
     own = core_ref.shape[0]
     rank = two_ref.shape[0]
+    bits = [n_rows >> (k + 1) for k in range(n_rows.bit_length() - 1)]
     chunks = n_i // STEP
     wide = GROUP * rank
 
@@ -50,10 +55,8 @@
         return pltpu.make_async_copy(q_hbm.at[rows], q_ref.at[rows], q_sem.at[c])
 
     barrier = pltpu.get_barrier_semaphore()
-    for d in range(1, n_rows):
-        pl.semaphore_signal(
-            barrier, inc=1, device_id={"rows": lax.rem(row + d, n_rows), "cols": col}, device_id_type=MESH
-        )
+    for bit in bits:
+        pl.semaphore_signal(barrier, inc=1, device_id={"rows": flip(row, bit), "cols": col}, device_id_type=MESH)
     for d in range(1, n_cols):
         pl.semaphore_signal(
             barrier, inc=1, device_id={"rows": row, "cols": lax.rem(col + d, n_cols)}, device_id_type=MESH
@@ -76,13 +79,21 @@
     for c in range(chunks):
         chunk_copy(c).start()
 
-    def push(ref, size, send, recv, axis, d):
-        count, me = (n_rows, row) if axis == "rows" else (n_cols, col)
-        peer = lax.rem(me + d, count)
-        where = {"rows": peer, "cols": col} if axis == "rows" else {"rows": row, "cols": peer}
-        slot = ref.at[pl.ds(pl.multiple_of(me * size, size), size), :]
+    def push(ref, size, send, recv, d):
+        where = {"rows": row, "cols": lax.rem(col + d, n_cols)}
+        slot = ref.at[pl.ds(pl.multiple_of(col * size, size), size), :]
         return pltpu.make_async_remote_copy(
             src_ref=slot, dst_ref=slot, send_sem=send.at[d], recv_sem=recv.at[d], device_id=where, device_id_type=MESH
+        )
+
+    place = sum(lax.rem(row // bit, 2) * (n_rows // 2 // bit) for bit in bits)
+
+    def core_step(k):
+        size = (8 * own) << k
+        slot = cf_ref.at[pl.ds(pl.multiple_of((place // (1 << k)) * size, size), size), :]
+        return pltpu.make_async_remote_copy(
+            src_ref=slot, dst_ref=slot, send_sem=core_send.at[k], recv_sem=core_recv.at[k],
+            device_id={"rows": flip(row, bits[k]), "cols": col}, device_id_type=MESH,
         )
 
     which = lax.broadcasted_iota(jnp.int32, pick_ref.shape, 1) // rank
@@ -92,7 +103,7 @@
     small[0].wait()
     for q in range(own):
         packed = jnp.concatenate([core_ref[q, 8 * b : 8 * b + 8, :] for b in range(4)], axis=1)
-        cf_ref[pl.ds(pl.multiple_of((row * own + q) * 8, 8), 8), :] = packed
+        cf_ref[pl.ds(pl.multiple_of((place * own + q) * 8, 8), 8), :] = packed
     for copy in small[1:]:
         copy.wait()
     wanted = jnp.full((rank, SLAB), slab_ref[0], jnp.int32)
@@ -110,10 +121,11 @@
     gram = lax.dot_general(two, two, NT, preferred_element_type=jnp.float32)
     gram_ref[pl.ds(pl.multiple_of(col * rank, rank), rank), :] = gram
 
-    pl.semaphore_wait(barrier, n_rows + n_cols - 2)
-    cores = [push(cf_ref, 8 * own, core_send, core_recv, "rows", d) for d in range(1, n_rows)]
-    grams = [push(gram_ref, rank, gram_send, gram_recv, "cols", d) for d in range(1, n_cols)]
-    for copy in grams + cores:
+    pl.semaphore_wait(barrier, len(bits) + n_cols - 1)
+    grams = [push(gram_ref, rank, gram_send, gram_recv, d) for d in range(1, n_cols)]
+    cores = [core_step(k) for k in range(len(bits))]
+    cores[0].start()
+    for copy in grams:
         copy.start()
 
     def chunk(c, carry):
@@ -139,19 +151,28 @@
                 pf_ref[pl.ds(start, 32), :] = jnp.concatenate(turned, axis=0)
         return carry
 
-    lax.fori_loop(0, chunks, chunk, 0)
-
-    for copy in cores:
-        copy.wait_recv()
+    early = min(len(bits) - 1, chunks)
+    for c in range(chunks):
+        chunk(c, 0)
+        if c < early:
+            cores[c].wait_recv()
+            cores[c + 1].start()
+    for k in range(early, len(bits)):
+        cores[k].wait_recv()
+        if k + 1 < len(bits):
+            cores[k + 1].start()
+    for r in range(n_rows):
+        slot = sum(r // bit % 2 * (n_rows // 2 // bit) for bit in bits)
+        core_all_ref[8 * own * r : 8 * own * (r + 1), :] = cf_ref[8 * own * slot : 8 * own * (slot + 1), :]
 
     def flat(ref, count):
         return jnp.concatenate([ref[pl.ds(a, count, stride=8), :] for a in range(8)], axis=1)
 
-    core_flat = flat(cf_ref, rank)
+    core_flat = flat(core_all_ref, rank)
     target_ref[pl.ds(pl.multiple_of(col * rank, rank), rank), :] = lax.dot_general(
         core_flat, flat(pf_ref, n_i), NT, preferred_element_type=jnp.float32, precision=HIGHEST
     )
-    targets = [push(target_ref, rank, target_send, target_recv, "cols", d) for d in range(1, n_cols)]
+    targets = [push(target_ref, rank, target_send, target_recv, d) for d in range(1, n_cols)]
     for copy in targets:
         copy.start()
 
@@ -164,7 +185,7 @@
     for copy in grams:
         copy.wait_recv()
     gram_two = sum(gram_ref[c * rank : (c + 1) * rank, :] for c in range(1, n_cols)) + gram_ref[0:rank, :]
-    left = jnp.dot(cf_ref[...], gram_three, preferred_element_type=jnp.float32, precision=HIGHEST)
+    left = jnp.dot(core_all_ref[...], gram_three, preferred_element_type=jnp.float32, precision=HIGHEST)
     stacked = []
     for g in range(rank // 4):
         stacked.append(
@@ -207,21 +228,24 @@
     packed = jnp.zeros((8, 128), jnp.float32)
     for b in range(rank // 8):
         packed = jnp.where(lane == b, squares[8 * b : 8 * b + 8], packed)
-    square_ref[pl.ds(pl.multiple_of(row * 8, 8), 8), :] = packed
-    sums = [push(square_ref, 8, sq_send, sq_recv, "rows", d) for d in range(1, n_rows)]
-    for copy in sums:
+    sums = []
+    for k, bit in enumerate(bits):
+        square_ref[k, 0] = packed
+        copy = pltpu.make_async_remote_copy(
+            src_ref=square_ref.at[k, 0], dst_ref=square_ref.at[k, 1], send_sem=sq_send.at[k], recv_sem=sq_recv.at[k],
+            device_id={"rows": flip(row, bit), "cols": col}, device_id_type=MESH,
+        )
         copy.start()
-    for copy in sums:
         copy.wait_recv()
-    totals = square_ref[0:8, :]
-    for r in range(1, n_rows):
-        totals = totals + square_ref[8 * r : 8 * r + 8, :]
+        packed = packed + square_ref[k, 1]
+        sums.append(copy)
+    totals = packed
     spread = jnp.sqrt(totals / (n_i * n_rows) + 1e-06)
     for b in range(rank // 8):
         new_one_ref[8 * b : 8 * b + 8, :] = updated[8 * b : 8 * b + 8] / spread[:, b : b + 1]
-    place = lax.broadcasted_iota(jnp.int32, (8, 128), 0) + 8 * lane
+    index = lax.broadcasted_iota(jnp.int32, (8, 128), 0) + 8 * lane
     for q in range(own):
-        mine = jnp.where(place == row * own + q, spread, 0.0)
+        mine = jnp.where(index == row * own + q, spread, 0.0)
         mine = jnp.sum(jnp.sum(mine, axis=1, keepdims=True), axis=0, keepdims=True)
         new_core_ref[q] = core_ref[q] * mine
     for copy in cores + grams + targets + sums:
@@ -255,9 +279,10 @@
             pltpu.VMEM((n_i * 8, 128), f32),
             pltpu.VMEM((rank * 8, 128), f32),
             pltpu.VMEM((rank * 8, 128), f32),
+            pltpu.VMEM((rank * 8, 128), f32),
             pltpu.VMEM((n_cols * rank, rank), f32),
             pltpu.VMEM((n_cols * rank, n_i), f32),
-            pltpu.VMEM((n_rows * 8, 128), f32),
+            pltpu.VMEM((n_rows.bit_length(), 2, 8, 128), f32),
             dma((5,)),
             dma((n_i // STEP,)),
             dma((n_rows,)),
@@ -270,9 +295,15 @@
             dma((n_rows,)),
         ],
         compiler_params=pltpu.CompilerParams(
-            collective_id=0, has_side_effects=True, vmem_limit_bytes=64 * 1024 * 1024
+            collective_id=0, has_side_effects=True, vmem_limit_bytes=40 * 1024 * 1024
         ),
-    )(slab_index, quantized, scales, mode_one.T, mode_two.T, mode_three.T, core_tensor)
+    )(
+        slab_index,
+        *(
+            pltpu.with_memory_space_constraint(x, pltpu.HBM)
+            for x in (quantized, scales, mode_one.T, mode_two.T, mode_three.T, core_tensor)
+        ),
+    )
     return one_t.T, new_core
 
 

time: 26.9 us -> 36 us (1.34)
  Pallas kernels: 22.6 us -> 33.3 us
  local copies, waits for them, and re-layouts: 2.75 us -> 1.23 us
    pallas_call x1, Pallas kernels: 22.6 us -> 33.3 us  [local(): pl.pallas_call(functools.partial(kernel, n_rows, n_cols), out_shape=(jax....]
    unnamed x2, local copies, waits for them, and re-layouts: 2.75 us -> 1.23 us
where the time goes in v3:
time: 36 us; the launch traced here: 35.8 us
  Pallas kernels  33.3 us (92%)
  between operations  1.29 us (4%)
  local copies, waits for them, and re-layouts  1.23 us (3%)
    pallas_call x1, Pallas kernels, local(): pl.pallas_call(functools.partial(kernel, n_rows, n_cols), out_shape=(jax....  33.3 us
    unnamed x2, local copies, waits for them, and re-layouts  1.23 us

profile of v3, /device:TPU:0, one launch (start us, length us, event | category | flops | bytes accessed | tf_op | source)
XLA Modules:
  0.0 35.8 jit_solution(9959234391687864150)
XLA Ops:
  1.3 33.3 %shard_map.86 = (f32[32,192]{1,0:T(8,128)S(1)}, f32[2,32,32]{2,1,0:T(8,128)S(1)}) custom-call(s32[1]{0:T(128)S(6)} %copy.11.slab_ref, bf16[192,192,128]{2,1,0:T(8,128)(2,1)} %q_hbm.1, bf16[192,192]{1,0:T(8,128)(2,1)} %scales_hbm.1, f32[32,192]{1,0:T(8,128)} %bitcast.6, bf16[32,192]{1,0:T(8,128)(2,1)} %bitcast.7, bf16[32,4096]{1,0:T(8,128)(2,1)} %bitcast.5, ...), custom_call_target="tpu_custom_call" | custom-call | tf_op jit(solution)/shard_map/pallas_call | solution.py:262
  34.6 0.6 %copy.12 = f32[192,32]{0,1:T(8,128)} copy(f32[192,32]{0,1:T(8,128)S(1)} %bitcast.4) | data formatting | bytes 49152
  35.2 0.6 %copy.13 = f32[2,32,32]{2,1,0:T(8,128)} copy(f32[2,32,32]{2,1,0:T(8,128)S(1)} %get-tuple-element.9) | data formatting | bytes 16384

commit v4 on v2

--- a/solution.py
+++ b/solution.py
@@ -270,9 +270,15 @@
             dma((n_rows,)),
         ],
         compiler_params=pltpu.CompilerParams(
-            collective_id=0, has_side_effects=True, vmem_limit_bytes=64 * 1024 * 1024
+            collective_id=0, has_side_effects=True, vmem_limit_bytes=40 * 1024 * 1024
         ),
-    )(slab_index, quantized, scales, mode_one.T, mode_two.T, mode_three.T, core_tensor)
+    )(
+        slab_index,
+        *(
+            pltpu.with_memory_space_constraint(x, pltpu.HBM)
+            for x in (quantized, scales, mode_one.T, mode_two.T, mode_three.T, core_tensor)
+        ),
+    )
     return one_t.T, new_core
 
 

time: 26.9 us -> 24.7 us (0.918)
  local copies, waits for them, and re-layouts: 2.75 us -> 1.23 us
  Pallas kernels: 22.6 us -> 22 us
    unnamed x2, local copies, waits for them, and re-layouts: 2.75 us -> 1.23 us
    pallas_call x1, Pallas kernels: 22.6 us -> 22 us  [local(): pl.pallas_call(functools.partial(kernel, n_rows, n_cols), out_shape=(jax....]
where the time goes in v4:
time: 24.7 us; the launch traced here: 24.5 us
  Pallas kernels  22 us (89%)
  between operations  1.29 us (5%)
  local copies, waits for them, and re-layouts  1.23 us (5%)
    pallas_call x1, Pallas kernels, local(): pl.pallas_call(functools.partial(kernel, n_rows, n_cols), out_shape=(jax....  22 us
    unnamed x2, local copies, waits for them, and re-layouts  1.23 us

profile of v4, /device:TPU:0, one launch (start us, length us, event | category | flops | bytes accessed | tf_op | source)
XLA Modules:
  0.0 24.5 jit_solution(12094003129990830302)
XLA Ops:
  1.3 22.0 %shard_map.86 = (f32[32,192]{1,0:T(8,128)S(1)}, f32[2,32,32]{2,1,0:T(8,128)S(1)}) custom-call(s32[1]{0:T(128)S(6)} %copy.11.slab_ref, bf16[192,192,128]{2,1,0:T(8,128)(2,1)} %q_hbm.1, bf16[192,192]{1,0:T(8,128)(2,1)} %scales_hbm.1, f32[32,192]{1,0:T(8,128)} %bitcast.6, bf16[32,192]{1,0:T(8,128)(2,1)} %bitcast.7, bf16[32,4096]{1,0:T(8,128)(2,1)} %bitcast.5, ...), custom_call_target="tpu_custom_call" | custom-call | tf_op jit(solution)/shard_map/pallas_call | solution.py:238
  23.3 0.6 %copy.12 = f32[192,32]{0,1:T(8,128)} copy(f32[192,32]{0,1:T(8,128)S(1)} %bitcast.4) | data formatting | bytes 49152
  23.9 0.6 %copy.13 = f32[2,32,32]{2,1,0:T(8,128)} copy(f32[2,32,32]{2,1,0:T(8,128)S(1)} %get-tuple-element.9) | data formatting | bytes 16384
